TPU v7x, 32 devices: a whole 2x2x4 slice. The times are simulated.
32 devices in a mesh: facet: 8 (over y, x, core), col: 4 (over z).
Axes of the slice: x: 2, y: 2, z: 4, core: 2. Of those that a mesh axis runs over, the one named last changes fastest.
Arguments:
- facets: float32 [2, 8, 24, 2, 4096], P(None, 'facet', None, None, 'col'), may hold values from -6 to 6
- facet_x: int32 [8], P('facet'), may hold values from 0 to 32767
- facet_y: int32 [2], replicated, may hold values from 0 to 32767
- col_u: int32 [8], replicated, may hold values from 0 to 32767
- slot_col: int32 [4, 8], P('col'), may hold values from 0 to 1
- slot_v: int32 [4, 8], P('col'), may hold values from 0 to 32767
Outputs:
- subgrids: float32 [4, 8, 512, 1024], P('col', 'facet')
Inputs may be any that keep to these rules, and one draw needn't show every extreme that they name: `col_u`: offset in the image. `slot_col`: the subgrid's column is owner * 2 + this value. `slot_v`: offset in the image.
All inputs are finite; a program needn't handle non-finite values.
Results may differ from a plain program's by a relative error of at most 0.0003.
Values sent between devices are 32-bit elements; how exact they have to be, the bound alone decides.
A program may use at most 128 MiB of HBM per device.

v0:
```python
import math

import jax
import jax.numpy as jnp
from jax import lax
from jax.sharding import PartitionSpec as P

FS = 4096
SG = 512
COLS_DEV = 2
SLOTS = 1


def mulmod(first_factor, second_factor, modulus):
    upper = first_factor * (second_factor // 512) % modulus
    return (upper * 512 + first_factor * (second_factor % 512)) % modulus


def column_part(real_part, imag_part, shifted, table, col_u, img, count):
    turn = 2.0 * math.pi / img
    column_angle = mulmod(col_u[:, None], shifted[None, :], img).astype(jnp.float32) * turn
    cosine = jnp.cos(column_angle)[:, None, :]
    sine = jnp.sin(column_angle)[:, None, :]
    turned_real = real_part[None] * cosine + imag_part[None] * sine
    turned_imag = imag_part[None] * cosine - real_part[None] * sine
    local_rows = real_part.shape[0]
    width = real_part.shape[1]
    stacked = jnp.stack([turned_real, turned_imag]).reshape(-1, width)
    product = jnp.dot(
        stacked, table, precision=lax.Precision.HIGHEST, preferred_element_type=jnp.float32
    )
    product = product.reshape(2, count, local_rows, 2 * SG)
    from_real = product[0]
    from_imag = product[1]
    real_out = from_real[..., :SG] + from_imag[..., SG:]
    imag_out = from_imag[..., :SG] - from_real[..., SG:]
    return jnp.concatenate([real_out, imag_out], axis=-1)


def slot_term(owned, row_cells, img, column, shift_v):
    turn = 2.0 * math.pi / img
    v_cells = (shift_v + jnp.arange(SG, dtype=jnp.int32)) % img
    angle = mulmod(v_cells[:, None], row_cells[None, :], img).astype(jnp.float32) * turn
    cosine = jnp.cos(angle)
    sine = jnp.sin(angle)
    chosen = lax.dynamic_index_in_dim(owned, column, 0, keepdims=False)
    first = jnp.dot(
        cosine, chosen, precision=lax.Precision.HIGHEST, preferred_element_type=jnp.float32
    )
    second = jnp.dot(
        sine, chosen, precision=lax.Precision.HIGHEST, preferred_element_type=jnp.float32
    )
    real_out = first[:, :SG] + second[:, SG:]
    imag_out = first[:, SG:] - second[:, :SG]
    return jnp.concatenate([real_out, imag_out], axis=-1)


def per_device(facets, facet_x, facet_y, col_u, slot_col, slot_v):
    width = facets.shape[-1]
    band_rows = facets.shape[2]
    img = FS * lax.axis_size("facet")
    turn = 2.0 * math.pi / img
    x_start = lax.axis_index("col") * width
    real_part = facets[:, 0, :, 0, :].reshape(-1, width)
    imag_part = facets[:, 0, :, 1, :].reshape(-1, width)
    shifted = (facet_x[0] + x_start + jnp.arange(width, dtype=jnp.int32)) % img
    u_cells = jnp.arange(SG, dtype=jnp.int32)
    table_angle = mulmod(u_cells[None, :], shifted[:, None], img).astype(jnp.float32) * turn
    table = jnp.concatenate([jnp.cos(table_angle), jnp.sin(table_angle)], axis=1)
    owned = lax.psum_scatter(
        column_part(
            real_part, imag_part, shifted, table, col_u, img, COLS_DEV * lax.axis_size("col")
        ),
        "col",
        scatter_dimension=0,
        tiled=True,
    )
    total_rows = owned.shape[1]
    row_ids = jnp.arange(total_rows, dtype=jnp.int32)
    y_start = jnp.where(row_ids // band_rows == 0, facet_y[0], facet_y[1])
    row_cells = (y_start + row_ids % band_rows) % img
    scale = 1.0 / math.sqrt(2.0 * FS * band_rows * lax.axis_size("facet"))
    owner_cols = slot_col[0]
    owner_shift = slot_v[0]
    merged = lax.psum(owned, "facet")

    def own_slot(slot_id):
        return slot_term(merged, row_cells, img, owner_cols[slot_id], owner_shift[slot_id])

    first_slot = lax.axis_index("facet") * SLOTS
    summed = lax.map(own_slot, first_slot + jnp.arange(SLOTS, dtype=jnp.int32))
    return (summed * scale)[None]


def solution(mesh):
    placed = (
        P(None, "facet", None, None, "col"),
        P("facet"),
        P(),
        P(),
        P("col", None),
        P("col", None),
    )
    return jax.shard_map(
        per_device,
        mesh=mesh,
        in_specs=placed,
        out_specs=P("col", "facet", None, None),
        check_vma=False,
    )
```

profile of v0, /device:TPU:0, one launch (start us, length us, event | category | flops | bytes accessed | tf_op | source)
XLA Modules:
  0.0 140.9 jit_solution(5407549524900106008)
XLA Ops:
  6.5 0.0 reduce-scatter.2.cloned.1.call-start
  7.2 0.0 copy-start.3
  7.2 0.0 copy-start
  7.2 9.3 %fusion.16 = (f32[1024,512]{1,0:T(8,128)S(1)}, f32[1024,512]{1,0:T(8,128)S(1)}) fusion(s32[1024]{0:T(1024)S(1)} %get-tuple-element.42, s32[1024]{0:T(1024)S(1)} %get-tuple-element.43), kind=kLoop, calls=%fused_computation.29 | loop fusion | flops 14680064 | bytes 4202496 | tf_op jit(solution)/shard_map/cos | solution.py:69
  16.5 0.0 copy-done.3
  16.5 0.2 fusion.40
  16.8 0.0 copy-done
  16.8 0.3 fusion.62
  17.2 0.4 multiply_add_fusion
  17.6 0.4 pad_maximum_fusion
  18.0 10.6 %fusion = f32[768,1024]{1,0:T(8,128)S(1)} fusion(f32[768,1024]{1,0:T(8,128)S(1)} %bitcast.23, f32[1024,512]{1,0:T(8,128)S(1)} %get-tuple-element.39, f32[1024,512]{1,0:T(8,128)S(1)} %get-tuple-element.38), kind=kOutput, calls=%fused_computation | convolution fusion | flops 9664724992 | bytes 10485760 | tf_op jit(solution)/shard_map/dot_general | solution.py:29
  28.6 0.4 fusion.61
  29.0 0.3 slice_add_fusion.1
  29.3 0.0 copy-start.4
  29.4 0.0 copy-start.5
  29.4 0.0 copy-start.2
  29.4 1.3 pad_maximum_fusion.1
  30.7 0.0 reduce-scatter.2.cloned.1.call-update
  30.7 0.3 all-reduce.2.cloned.1.call-start
  31.0 0.0 copy-done.4
  31.0 0.0 copy-done.5
  31.0 0.6 constant_dynamic-slice_fusion
  33.5 0.6 fusion.63
  34.1 34.9 %reduce-scatter.2.cloned.1.call-done = f32[2,48,1024]{2,1,0:T(8,128)} async-done(((f32[8,48,1024]{2,1,0:T(8,128)}), f32[2,48,1024]{2,1,0:T(8,128)}) %reduce-scatter.2.cloned.1.call-update) | async-done | bytes 393232 | tf_op jit(solution)/shard_map/reduce_scatter | solution.py:70
  69.0 0.0 all-reduce.2.cloned.1.call-update
  69.0 1.2 and_select_fusion
  70.2 0.6 add_select_fusion.9
  70.9 54.4 %all-reduce.2.cloned.1.call-done = f32[2,48,1024]{2,1,0:T(8,128)} async-done(((f32[2,48,1024]{2,1,0:T(8,128)}), f32[2,48,1024]{2,1,0:T(8,128)}) %all-reduce.2.cloned.1.call-update) | async-done | bytes 393232 | tf_op jit(solution)/shard_map/psum | solution.py:85
  125.3 3.8 %fusion.25 = f32[512,1024]{1,0:T(8,128)S(1)} fusion(f32[2,48,1024]{2,1,0:T(8,128)} %all-reduce.2.cloned.1.call-done, s32[]{:T(128)S(6)} %select_n.215, s32[48]{0:T(128)S(1)} %get-tuple-element.44, s32[48]{0:T(128)S(1)} %get-tuple-element.45, s32[512]{0:T(512)S(1)} %add_select_fusion.9), kind=kOutput, calls=%fused_computation.48 | convolution fusion | flops 302678016 | bytes 2296196 | tf_op jit(solution)/shard_map/while/body/eval_jaxpr/dot_general | solution.py:47
  129.2 2.8 %fusion.23 = f32[512,1024]{1,0:T(8,128)S(1)} fusion(f32[2,48,1024]{2,1,0:T(8,128)S(1)} %copy-done.1, s32[]{:T(128)S(6)} %select_n.215, s32[48]{0:T(128)S(1)} %get-tuple-element.44, s32[48]{0:T(128)S(1)} %get-tuple-element.45, s32[512]{0:T(512)S(1)} %add_select_fusion.9), kind=kOutput, calls=%fused_computation.46 | convolution fusion | flops 302678016 | bytes 2296836 | tf_op jit(solution)/shard_map/while/body/eval_jaxpr/dot_general | solution.py:50
  132.0 0.5 fusion.14
  132.5 1.5 %maximum_multiply_fusion = f32[1,1,512,1024]{3,2,1,0:T(8,128)} fusion(f32[1,1,512,512]{3,2,1,0:T(8,128)S(1)} %get-tuple-element.18, f32[1,1,512,512]{3,2,1,0:T(8,128)S(1)} %get-tuple-element.17), kind=kLoop, calls=%fused_computation.17 | loop fusion | flops 1048576 | bytes 4194304 | tf_op jit(solution)/shard_map/mul | solution.py:92
  (6 shorter events, 0.1 us)
Async XLA Ops:
  6.5 62.5 %reduce-scatter.2.cloned.1.call-start = ((), (), s32[]{:S(2)}) async-start(), calls=%async_computation.1 | async-start | bytes 1966080 | tf_op jit(solution)/shard_map/reduce_scatter | solution.py:70
  7.2 9.3 %copy-start.3 = (s32[8]{0:T(128)S(1)}, s32[8]{0:T(128)}, u32[]{:S(2)}) copy-start(s32[8]{0:T(128)} %param.9) | copy-start | bytes 100
  7.2 9.6 %copy-start = (f32[2,1,24,2,1024]{4,3,2,1,0:T(2,128)S(1)}, f32[2,1,24,2,1024]{4,3,2,1,0:T(2,128)}, u32[]{:S(2)}) copy-start(f32[2,1,24,2,1024]{4,3,2,1,0:T(2,128)} %param.6) | copy-start | bytes 1179652
  29.3 1.6 %copy-start.4 = (s32[1,8]{1,0:T(1,128)S(1)}, s32[1,8]{1,0:T(1,128)}, u32[]{:S(2)}) copy-start(s32[1,8]{1,0:T(1,128)} %param.10) | copy-start | bytes 100
  29.4 1.6 %copy-start.5 = (s32[1,8]{1,0:T(1,128)S(1)}, s32[1,8]{1,0:T(1,128)}, u32[]{:S(2)}) copy-start(s32[1,8]{1,0:T(1,128)} %param.11) | copy-start | bytes 100
  29.4 4.1 %copy-start.2 = (s32[2]{0:T(128)S(1)}, s32[2]{0:T(128)}, u32[]{:S(2)}) copy-start(s32[2]{0:T(128)} %param.8) | copy-start | bytes 28
  30.7 94.6 %all-reduce.2.cloned.1.call-start = ((), (), s32[]{:S(2)}) async-start(), calls=%async_computation.2 | async-start | bytes 786432 | tf_op jit(solution)/shard_map/psum | solution.py:85
  125.3 3.8 %copy-start.1 = (f32[2,48,1024]{2,1,0:T(8,128)S(1)}, f32[2,48,1024]{2,1,0:T(8,128)}, u32[]{:S(2)}) copy-start(f32[2,48,1024]{2,1,0:T(8,128)} %all-reduce.2.cloned.1.call-done) | copy-start | bytes 1179652
Sparse Core Ops, SparseCore 0:
  30.8 38.1 reduce-scatter.1
  72.1 53.2 all-reduce.1
where the time goes:
time: 141 us
  waiting for transfers between devices  89.4 us (63%)
  matrix products  17.2 us (12%)
  between operations  16.2 us (11%)
  other arithmetic  15.9 us (11%)
  local copies, waits for them, and re-layouts  1.98 us (1%)
    psum x1, waiting for transfers between devices, per_device(): merged = lax.psum(owned, 'facet')  54.4 us
    reduce_scatter x1, waiting for transfers between devices, per_device(): lax.psum_scatter(column_part(real_part, imag_part, shifted, table, col_u,...  34.9 us
    dot_general x1, matrix products, column_part(): jnp.dot(stacked, table, precision=lax.Precision.HIGHEST, preferred_elemen...  10.6 us
    cos x1, other arithmetic, per_device(): jnp.cos(table_angle)  9.29 us
    dot_general x1, matrix products, slot_term(): jnp.dot(cosine, chosen, precision=lax.Precision.HIGHEST, preferred_elemen...  3.81 us
    dot_general x1, matrix products, slot_term(): jnp.dot(sine, chosen, precision=lax.Precision.HIGHEST, preferred_element_...  2.82 us
  transfers between devices with their start and end apart: 2, of which 2 were waited for; matrix products, arithmetic and copies ran while one was open for 2% of the time, Pallas kernels for 0%

commit v1 on v0

v1 whole, which is shorter than its diff:
```python
import functools
import math

import jax
import jax.numpy as jnp
from jax import lax
from jax.experimental import pallas as pl
from jax.experimental.pallas import tpu as pltpu
from jax.sharding import PartitionSpec as P

SG = 512
HALF = SG // 2
COLS_DEV = 2
F32 = jnp.float32
BF16 = jnp.bfloat16
I32 = jnp.int32
MESH = pl.DeviceIdType.MESH


def turn(m, mod):
    bits = mod.bit_length() - 1
    m = m & (mod - 1)
    quad = lax.shift_right_logical(m + (mod >> 3), jnp.int32(bits - 2))
    rest = m - lax.shift_left(quad, jnp.int32(bits - 2))
    t = rest.astype(F32) * F32(2.0 * math.pi / mod)
    t2 = t * t
    sine = t + t * t2 * (F32(-1 / 6) + t2 * (F32(1 / 120) + t2 * F32(-1 / 5040)))
    cosine = F32(1.0) + t2 * (
        F32(-0.5) + t2 * (F32(1 / 24) + t2 * (F32(-1 / 720) + t2 * F32(1 / 40320)))
    )
    odd = (quad & 1) == 1
    c = jnp.where(odd, sine, cosine)
    s = jnp.where(odd, cosine, sine)
    c = jnp.where(((quad + 1) & 2) == 2, -c, c)
    s = jnp.where((quad & 2) == 2, -s, s)
    return c, s


def split(value):
    high = value.astype(BF16)
    return high, (value - high.astype(F32)).astype(BF16)


def mm(a, b):
    return jnp.dot(a, b, preferred_element_type=F32)


def gather_kernel(
    nf, nc, img, band,
    fx_ref, fy_ref, u_ref, sc_ref, sv_ref, ucol_ref, facets_ref,
    h_ref, e_ref,
    cells, fxs, fxall, table, premod, zbuf, part, zrecv, total, gat,
    s_a2a, r_a2a, s_fx, r_fx, s_z, r_z, s_g, r_g, l_sem,
):
    f = lax.axis_index("facet")
    c = lax.axis_index("col")
    rows = facets_ref.shape[0]
    rpd = rows // nf
    width = facets_ref.shape[-1]
    mod = 2 * img
    ncell = COLS_DEV * rpd
    pad = h_ref.shape[0] // nf

    fxs[...] = jnp.full(fxs.shape, fx_ref[0], I32)
    barrier = pltpu.get_barrier_semaphore()
    for d in range(1, nf):
        pl.semaphore_signal(barrier, inc=1, device_id=(lax.rem(f + d, nf), c), device_id_type=MESH)
    for d in range(1, nc):
        pl.semaphore_signal(barrier, inc=1, device_id=(f, lax.rem(c + d, nc)), device_id_type=MESH)
    pl.semaphore_wait(barrier, nf + nc - 2)

    sends = []
    for d in range(1, nf):
        peer = lax.rem(f + d, nf)
        copy = pltpu.make_async_remote_copy(
            src_ref=facets_ref.at[pl.ds(peer * rpd, rpd)],
            dst_ref=cells.at[:, :, f],
            send_sem=s_a2a.at[d], recv_sem=r_a2a.at[d],
            device_id=(peer, c), device_id_type=MESH,
        )
        copy.start()
        small = pltpu.make_async_remote_copy(
            src_ref=fxs, dst_ref=fxall.at[f],
            send_sem=s_fx.at[d], recv_sem=r_fx.at[d],
            device_id=(peer, c), device_id_type=MESH,
        )
        small.start()
        sends += [copy, small]
    own = pltpu.make_async_copy(facets_ref.at[pl.ds(f * rpd, rpd)], cells.at[:, :, f], l_sem.at[0])
    own.start()
    own_fx = pltpu.make_async_copy(fxs, fxall.at[f], l_sem.at[1])
    own_fx.start()

    start = c * width
    block = 64

    def table_step(i, carry):
        first = pl.multiple_of(i * block, block)
        x = lax.broadcasted_iota(I32, (block, HALF), 0) + (start + first)
        j = lax.broadcasted_iota(I32, (block, HALF), 1)
        cosine, sine = turn((2 * j + 1) * x, mod)
        ch, cl = split(cosine)
        sh, sl = split(sine)
        table[0, pl.ds(first, block), pl.ds(0, HALF)] = ch
        table[0, pl.ds(first, block), pl.ds(HALF, HALF)] = sh
        table[1, pl.ds(first, block), pl.ds(0, HALF)] = cl
        table[1, pl.ds(first, block), pl.ds(HALF, HALF)] = sl
        return carry

    lax.fori_loop(0, width // block, table_step, 0)
    ucol = ucol_ref[...]
    xs = lax.broadcasted_iota(I32, (ucol.shape[0], width), 1) + start
    pc, ps = turn((2 * ucol + (SG - 1)) * xs, mod)
    premod[0] = pc
    premod[1] = ps

    scale = 1.0 / math.sqrt(1.0 * rows * width * nc * nf)
    shift_v = jnp.full((1, 1), sv_ref[f], I32)
    chosen = jnp.full((1, 1), sc_ref[f], I32)
    fy0 = jnp.full((1, 1), fy_ref[0], I32)
    fy1 = jnp.full((1, 1), fy_ref[1], I32)

    def v_step(i, carry):
        first = pl.multiple_of(i * block, block)
        b = lax.broadcasted_iota(I32, (block, nf * pad), 0) + first
        q = lax.broadcasted_iota(I32, (1, nf * pad), 1)
        inner = lax.rem(q, pad)
        peer = lax.div(q, pad)
        column = lax.div(inner, rpd)
        g = peer * rpd + lax.rem(inner, rpd)
        cell = jnp.where(g < band, fy0 + g, fy1 + g - band)
        use = (inner < ncell) & (column == chosen)
        cosine, sine = turn(2 * (shift_v + b) * cell, mod)
        weight = jnp.where(use, F32(scale), F32(0.0))
        e_ref[pl.ds(first, block), pl.ds(0, nf * pad)] = cosine * weight
        e_ref[pl.ds(first, block), pl.ds(nf * pad, nf * pad)] = sine * weight
        return carry

    lax.fori_loop(0, SG // block, v_step, 0)
    h_ref[...] = jnp.zeros_like(h_ref)

    own.wait()
    own_fx.wait()
    for copy in sends:
        copy.wait()

    fx = fxall[:, 0, :]
    fx = jnp.concatenate([fx] * (SG // fx.shape[-1]), axis=1)
    lane = lax.broadcasted_iota(I32, (nf, SG), 1)
    a = jnp.where(lane < HALF, HALF + lane, SG - 1 - lane)

    zcopies = []
    for d in list(range(1, nc)) + [0]:
        owner = lax.rem(c + d, nc)
        for s in range(COLS_DEV):
            col = owner * COLS_DEV + s
            cosine = premod[0, pl.ds(col, 1), :].reshape(1, 1, width)
            sine = premod[1, pl.ds(col, 1), :].reshape(1, 1, width)
            re = cells[:, 0]
            im = cells[:, 1]
            zr = (re * cosine + im * sine).reshape(rpd * nf, width)
            zi = (im * cosine - re * sine).reshape(rpd * nf, width)
            for n, z in enumerate((zr, zi)):
                hi, lo = split(z)
                at = (s * 2 + n) * rpd * nf
                zbuf[0, pl.ds(at, rpd * nf), :] = hi
                zbuf[1, pl.ds(at, rpd * nf), :] = lo
        prod = mm(zbuf[0], table[0]) + mm(zbuf[1], table[0]) + mm(zbuf[0], table[1])
        for s in range(COLS_DEV):
            col = owner * COLS_DEV + s
            at = s * 2 * rpd * nf
            fr = prod[at:at + rpd * nf]
            fi = prod[at + rpd * nf:at + 2 * rpd * nf]
            rc, rs = fr[:, :HALF], fr[:, HALF:]
            ic, is_ = fi[:, :HALF], fi[:, HALF:]
            hr = jnp.concatenate([rc + is_, rc - is_], axis=1).reshape(rpd, nf, SG)
            hm = jnp.concatenate([ic - rs, ic + rs], axis=1).reshape(rpd, nf, SG)
            wc, ws = turn(2 * (a + u_ref[col]) * fx, mod)
            out_r = jnp.sum(hr * wc + hm * ws, axis=1)
            out_i = jnp.sum(hm * wc - hr * ws, axis=1)
            part[d, pl.ds(s * rpd, rpd), pl.ds(0, SG)] = out_r
            part[d, pl.ds(s * rpd, rpd), pl.ds(SG, SG)] = out_i
        if d:
            copy = pltpu.make_async_remote_copy(
                src_ref=part.at[d], dst_ref=zrecv.at[d],
                send_sem=s_z.at[d], recv_sem=r_z.at[d],
                device_id=(f, owner), device_id_type=MESH,
            )
            copy.start()
            zcopies.append(copy)

    acc = part[0]
    for d, copy in zip(range(1, nc), zcopies):
        copy.wait()
        acc = acc + zrecv[d]
    flip = lax.broadcasted_iota(I32, (HALF, HALF), 0) + lax.broadcasted_iota(I32, (HALF, HALF), 1)
    flip = jnp.where(flip == HALF - 1, F32(1.0), F32(0.0)).astype(BF16)
    for n in range(2):
        low = acc[:, n * SG + HALF:(n + 1) * SG]
        hi, lo = split(low)
        total[:, pl.ds(n * SG, HALF)] = mm(hi, flip) + mm(lo, flip)
        total[:, pl.ds(n * SG + HALF, HALF)] = acc[:, n * SG:n * SG + HALF]

    gcopies = []
    for d in range(1, nf):
        peer = lax.rem(f + d, nf)
        copy = pltpu.make_async_remote_copy(
            src_ref=total, dst_ref=gat.at[f],
            send_sem=s_g.at[d], recv_sem=r_g.at[d],
            device_id=(peer, c), device_id_type=MESH,
        )
        copy.start()
        gcopies.append(copy)
    own = pltpu.make_async_copy(total, gat.at[f], l_sem.at[2])
    own.start()
    own.wait()
    for copy in gcopies:
        copy.wait()
    for j in range(nf):
        h_ref[pl.ds(j * pad, ncell), :] = gat[j]


def v_kernel(h_ref, e_ref, out_ref, rhs_hi, rhs_lo):
    @pl.when(pl.program_id(0) == 0)
    def _():
        k = h_ref.shape[0]
        hi, lo = split(h_ref[...])
        for ref, h in ((rhs_hi, hi), (rhs_lo, lo)):
            ref[pl.ds(0, k), :] = h
            ref[pl.ds(k, k), pl.ds(0, SG)] = h[:, SG:]
            ref[pl.ds(k, k), pl.ds(SG, SG)] = -h[:, :SG]

    eh, el = split(e_ref[...])
    out_ref[...] = mm(eh, rhs_hi[...]) + mm(el, rhs_hi[...]) + mm(eh, rhs_lo[...])


def per_device(nf, nc, facets, facet_x, facet_y, col_u, slot_col, slot_v):
    width = facets.shape[-1]
    band = facets.shape[2]
    img = width * nc * nf
    rows = facets.shape[0] * band
    rpd = rows // nf
    ncol = COLS_DEV * nc
    ncell = COLS_DEV * rpd
    pad = -(-ncell // 16) * 16
    vm = pl.BlockSpec(memory_space=pltpu.VMEM)
    sm = pl.BlockSpec(memory_space=pltpu.SMEM)
    dma = pltpu.SemaphoreType.DMA
    h, e = pl.pallas_call(
        functools.partial(gather_kernel, nf, nc, img, band),
        out_shape=(
            jax.ShapeDtypeStruct((nf * pad, 2 * SG), F32),
            jax.ShapeDtypeStruct((SG, 2 * nf * pad), F32),
        ),
        in_specs=[sm, sm, sm, sm, sm, vm, pl.BlockSpec(memory_space=pl.ANY)],
        out_specs=(vm, vm),
        scratch_shapes=[
            pltpu.VMEM((rpd, 2, nf, width), F32),
            pltpu.VMEM((8, 128), I32),
            pltpu.VMEM((nf, 8, 128), I32),
            pltpu.VMEM((2, width, SG), BF16),
            pltpu.VMEM((2, ncol, width), F32),
            pltpu.VMEM((2, 2 * COLS_DEV * rpd * nf, width), BF16),
            pltpu.VMEM((nc, ncell, 2 * SG), F32),
            pltpu.VMEM((nc, ncell, 2 * SG), F32),
            pltpu.VMEM((ncell, 2 * SG), F32),
            pltpu.VMEM((nf, ncell, 2 * SG), F32),
            dma((nf,)), dma((nf,)), dma((nf,)), dma((nf,)),
            dma((nc,)), dma((nc,)), dma((nf,)), dma((nf,)), dma((3,)),
        ],
        compiler_params=pltpu.CompilerParams(collective_id=0, has_side_effects=True),
        name="gather_columns",
    )(
        facet_x, facet_y, col_u, slot_col[0], slot_v[0], col_u[:, None],
        facets.reshape(rows, 2, width),
    )
    tile = 128
    out = pl.pallas_call(
        v_kernel,
        grid=(SG // tile,),
        out_shape=jax.ShapeDtypeStruct((SG, 2 * SG), F32),
        in_specs=[
            pl.BlockSpec((nf * pad, 2 * SG), lambda i: (0, 0)),
            pl.BlockSpec((tile, 2 * nf * pad), lambda i: (i, 0)),
        ],
        out_specs=pl.BlockSpec((tile, 2 * SG), lambda i: (i, 0)),
        scratch_shapes=[
            pltpu.VMEM((2 * nf * pad, 2 * SG), BF16),
            pltpu.VMEM((2 * nf * pad, 2 * SG), BF16),
        ],
        name="v_transform",
    )(h, e)
    return out[None, None]


def solution(mesh):
    placed = (
        P(None, "facet", None, None, "col"),
        P("facet"),
        P(),
        P(),
        P("col", None),
        P("col", None),
    )
    return jax.shard_map(
        functools.partial(per_device, mesh.shape["facet"], mesh.shape["col"]),
        mesh=mesh,
        in_specs=placed,
        out_specs=P("col", "facet", None, None),
        check_vma=False,
    )
```

time: 141 us -> 36 us (0.26)
  waiting for transfers between devices: 89.4 us -> 0 us
  Pallas kernels: 0 us -> 33.7 us
  matrix products: 17.2 us -> 0 us
  other arithmetic: 15.9 us -> 0 us
  between operations: 16.2 us -> 0.66 us
    psum x1 -> x0, waiting for transfers between devices: 54.4 us -> none  [per_device(): merged = lax.psum(owned, 'facet')]
    reduce_scatter x1 -> x0, waiting for transfers between devices: 34.9 us -> none  [per_device(): lax.psum_scatter(column_part(real_part, imag_part, shifted, table, col_u,...]
    pallas_call x0 -> x2, Pallas kernels: none -> 33.7 us  [the longest x1 29.2 us: per_device(): pl.pallas_call(functools.partial(gather_kernel, nf, nc, img, band), out_s...]
    dot_general x3 -> x0, matrix products: 17.2 us -> none  [the longest x1 10.6 us: column_part(): jnp.dot(stacked, table, precision=lax.Precision.HIGHEST, preferred_elemen...]
    cos x2 -> x0, other arithmetic: 9.52 us -> none  [the longest x1 9.29 us: per_device(): jnp.cos(table_angle)]
    select_n x3 -> x0, other arithmetic: 1.88 us -> none  [the longest x2 1.24 us: mulmod(): return (upper * 512 + first_factor * (second_factor % 512)) % modulus]
    concatenate x2 -> x0, other arithmetic: 1.76 us -> none  [the longest x1 1.28 us: column_part(): return jnp.concatenate([real_out, imag_out], axis=-1)]
    mul x1 -> x0, other arithmetic: 1.53 us -> none  [per_device(): return (summed * scale)[None]]
  transfers between devices with their start and end apart: 2 -> 0, of which waited for: 2 -> 0; matrix products, arithmetic and copies ran while one was open for 2% -> 0% of each run, Pallas kernels for 0% -> 0%
where the time goes in v1:
time: 36 us; the launch traced here: 35.7 us
  Pallas kernels  33.7 us (94%)
  local copies, waits for them, and re-layouts  1.32 us (4%)
  between operations  0.66 us (2%)
    pallas_call x1, Pallas kernels, per_device(): pl.pallas_call(functools.partial(gather_kernel, nf, nc, img, band), out_s...  29.2 us
    pallas_call x1, Pallas kernels, per_device(): pl.pallas_call(v_kernel, grid=(SG // tile,), out_shape=jax.ShapeDtypeStru...  4.52 us
    broadcast_in_dim x1, local copies, waits for them, and re-layouts, per_device(): col_u[:, None]  1.32 us

profile of v1, /device:TPU:0, one launch (start us, length us, event | category | flops | bytes accessed | tf_op | source)
XLA Modules:
  0.0 35.7 jit_solution(11649264685790682457)
XLA Ops:
  0.7 1.3 %copy.7.ucol_ref = s32[8,1]{1,0:T(8,128)} copy(s32[8,1]{0,1:T(1,128)} %bitcast.6) | data formatting | bytes 64 | tf_op jit(solution)/shard_map/broadcast_in_dim | solution.py:274
  2.0 29.2 %gather_columns.1 = (f32[128,1024]{1,0:T(8,128)}, f32[512,256]{1,0:T(8,128)}) custom-call(s32[1]{0:T(128)S(6)} %copy.8.fx_ref, s32[2]{0:T(128)} %fy_ref.1, s32[8]{0:T(128)} %u_ref.1, s32[8]{0:T(128)} %bitcast.7, s32[8]{0:T(128)} %bitcast.8, s32[8,1]{1,0:T(8,128)} %copy.7.ucol_ref, f32[48,2,1024]{2,1,0:T(2,128)} %bitcast.5), custom_call_target="tpu_custom_call" | custom-call | tf_op jit(solution)/shard_map/gather_columns/pallas_call | solution.py:249
  31.2 4.5 %v_transform.1 = f32[512,1024]{1,0:T(8,128)} custom-call(f32[128,1024]{1,0:T(8,128)} %get-tuple-element.7.h_ref, f32[512,256]{1,0:T(8,128)} %get-tuple-element.8.e_ref), custom_call_target="tpu_custom_call" | custom-call | tf_op jit(solution)/shard_map/v_transform/pallas_call | solution.py:278

commit v2 on v1

v2 whole, which is shorter than its diff:
```python
import functools
import math

import jax
import jax.numpy as jnp
from jax import lax
from jax.experimental import pallas as pl
from jax.experimental.pallas import tpu as pltpu
from jax.sharding import PartitionSpec as P

SG = 512
HALF = SG // 2
COLS_DEV = 2
F32 = jnp.float32
BF16 = jnp.bfloat16
I32 = jnp.int32
MESH = pl.DeviceIdType.MESH


def turn(m, mod):
    bits = mod.bit_length() - 1
    m = m & (mod - 1)
    quad = lax.shift_right_logical(m + (mod >> 3), jnp.int32(bits - 2))
    rest = m - lax.shift_left(quad, jnp.int32(bits - 2))
    t = rest.astype(F32) * F32(2.0 * math.pi / mod)
    t2 = t * t
    sine = t + t * t2 * (F32(-1 / 6) + t2 * (F32(1 / 120) + t2 * F32(-1 / 5040)))
    cosine = F32(1.0) + t2 * (
        F32(-0.5) + t2 * (F32(1 / 24) + t2 * (F32(-1 / 720) + t2 * F32(1 / 40320)))
    )
    odd = (quad & 1) == 1
    c = jnp.where(odd, sine, cosine)
    s = jnp.where(odd, cosine, sine)
    c = jnp.where(((quad + 1) & 2) == 2, -c, c)
    s = jnp.where((quad & 2) == 2, -s, s)
    return c, s


def split(value):
    high = value.astype(BF16)
    return high, (value - high.astype(F32)).astype(BF16)


def mm(a, b):
    return jnp.dot(a, b, preferred_element_type=F32)


def partner(index, count, step):
    if count & (count - 1):
        return lax.rem(index + step, count)
    bit = 1
    while bit < count:
        if step & bit:
            index = index + bit - 2 * bit * lax.rem(lax.div(index, bit), 2)
        bit *= 2
    return index


def gather_kernel(
    nf, nc, img, band, cuts, hpad,
    fx_ref, fy_ref, u_ref, sc_ref, sv_ref, facets_ref,
    h_ref, e_ref,
    cells, fxs, fxall, table, premod, phase, zbuf, part, zrecv, gsend, gat,
    s_a2a, r_a2a, s_fx, r_fx, s_z, r_z, s_g, r_g, l_sem,
):
    f = lax.axis_index("facet")
    c = lax.axis_index("col")
    rows = facets_ref.shape[0]
    rpd = rows // nf
    width = facets_ref.shape[-1]
    mod = 2 * img
    ncol = COLS_DEV * nc
    depth = len(cuts) * nf * hpad

    fxs[...] = jnp.full(fxs.shape, fx_ref[0], I32)
    barrier = pltpu.get_barrier_semaphore()
    for d in range(1, nf):
        pl.semaphore_signal(barrier, inc=1, device_id=(partner(f, nf, d), c), device_id_type=MESH)
    for d in range(1, nc):
        pl.semaphore_signal(barrier, inc=1, device_id=(f, partner(c, nc, d)), device_id_type=MESH)

    start = c * width
    xs = lax.broadcasted_iota(I32, (ncol, width), 1) + start
    row = lax.broadcasted_iota(I32, (ncol, width), 0)
    uv = jnp.zeros((ncol, width), I32)
    for i in range(ncol):
        uv = jnp.where(row == i, u_ref[i], uv)
    pc, ps = turn((2 * uv + (SG - 1)) * xs, mod)
    premod[0] = pc
    premod[1] = ps
    h_ref[...] = jnp.zeros_like(h_ref)
    pl.semaphore_wait(barrier, nf + nc - 2)

    small = []
    sends = []
    for d in range(1, nf):
        copy = pltpu.make_async_remote_copy(
            src_ref=fxs, dst_ref=fxall.at[f],
            send_sem=s_fx.at[d], recv_sem=r_fx.at[d],
            device_id=(partner(f, nf, d), c), device_id_type=MESH,
        )
        copy.start()
        small.append(copy)
    copy = pltpu.make_async_copy(fxs, fxall.at[f], l_sem.at[len(cuts)])
    copy.start()
    small.append(copy)
    for n, (y0, ny) in enumerate(cuts):
        group = []
        for d in range(1, nf):
            peer = partner(f, nf, d)
            copy = pltpu.make_async_remote_copy(
                src_ref=facets_ref.at[pl.ds(peer * rpd + y0, ny)],
                dst_ref=cells.at[pl.ds(y0, ny), :, f],
                send_sem=s_a2a.at[n, d], recv_sem=r_a2a.at[n, d],
                device_id=(peer, c), device_id_type=MESH,
            )
            copy.start()
            group.append(copy)
        copy = pltpu.make_async_copy(
            facets_ref.at[pl.ds(f * rpd + y0, ny)], cells.at[pl.ds(y0, ny), :, f], l_sem.at[n]
        )
        copy.start()
        group.append(copy)
        sends.append(group)

    block = 64

    def table_step(i, carry):
        first = pl.multiple_of(i * block, block)
        x = lax.broadcasted_iota(I32, (block, HALF), 0) + (start + first)
        j = lax.broadcasted_iota(I32, (block, HALF), 1)
        cosine, sine = turn((2 * j + 1) * x, mod)
        ch, cl = split(cosine)
        sh, sl = split(sine)
        table[0, pl.ds(first, block), pl.ds(0, HALF)] = ch
        table[0, pl.ds(first, block), pl.ds(HALF, HALF)] = sh
        table[1, pl.ds(first, block), pl.ds(0, HALF)] = cl
        table[1, pl.ds(first, block), pl.ds(HALF, HALF)] = sl
        return carry

    lax.fori_loop(0, width // block, table_step, 0)

    for copy in small:
        copy.wait()
    fx = fxall[:, 0, :]
    fx = jnp.concatenate([fx] * (SG // fx.shape[-1]), axis=1)
    lane = lax.broadcasted_iota(I32, (nf, SG), 1)
    a = jnp.where(lane < HALF, HALF + lane, SG - 1 - lane)

    def phase_step(i, carry):
        wc, ws = turn(2 * (a + u_ref[i]) * fx, mod)
        phase[0, i] = wc
        phase[1, i] = ws
        return carry

    lax.fori_loop(0, ncol, phase_step, 0)

    def transform(n):
        y0, ny = cuts[n]
        size = ny * nf
        for d in list(range(nc - 1, 0, -1)) + [0]:
            owner = partner(c, nc, d)
            for s in range(COLS_DEV):
                col = owner * COLS_DEV + s
                cosine = premod[0, pl.ds(col, 1), :].reshape(1, 1, width)
                sine = premod[1, pl.ds(col, 1), :].reshape(1, 1, width)
                re = cells[pl.ds(y0, ny), 0]
                im = cells[pl.ds(y0, ny), 1]
                zr = (re * cosine + im * sine).reshape(size, width)
                zi = (im * cosine - re * sine).reshape(size, width)
                for m, z in enumerate((zr, zi)):
                    hi, lo = split(z)
                    at = (s * 2 + m) * size
                    zbuf[0, pl.ds(at, size), :] = hi
                    zbuf[1, pl.ds(at, size), :] = lo
            every = pl.ds(0, 2 * COLS_DEV * size)
            high = zbuf[0, every, :]
            prod = mm(high, table[0]) + mm(zbuf[1, every, :], table[0]) + mm(high, table[1])
            for s in range(COLS_DEV):
                col = owner * COLS_DEV + s
                at = s * 2 * size
                fr = prod[at:at + size]
                fi = prod[at + size:at + 2 * size]
                rc, rs = fr[:, :HALF], fr[:, HALF:]
                ic, is_ = fi[:, :HALF], fi[:, HALF:]
                hr = jnp.concatenate([rc + is_, rc - is_], axis=1).reshape(ny, nf, SG)
                hm = jnp.concatenate([ic - rs, ic + rs], axis=1).reshape(ny, nf, SG)
                wc = phase[0, col]
                ws = phase[1, col]
                part[n, d, pl.ds(s * ny, ny), pl.ds(0, SG)] = jnp.sum(hr * wc + hm * ws, axis=1)
                part[n, d, pl.ds(s * ny, ny), pl.ds(SG, SG)] = jnp.sum(hm * wc - hr * ws, axis=1)
            if d:
                copy = pltpu.make_async_remote_copy(
                    src_ref=part.at[n, d], dst_ref=zrecv.at[n, d],
                    send_sem=s_z.at[n, d], recv_sem=r_z.at[n, d],
                    device_id=(f, owner), device_id_type=MESH,
                )
                copy.start()
                zcopies[n].append((d, copy))

    scale = 1.0 / math.sqrt(1.0 * rows * width * nc * nf)

    def v_step(i, carry):
        first = pl.multiple_of(i * block, block)
        b = lax.broadcasted_iota(I32, (block, depth), 0) + first
        q = lax.broadcasted_iota(I32, (block, depth), 1)
        inner = lax.rem(q, hpad)
        peer = lax.rem(lax.div(q, hpad), nf)
        piece = lax.div(q, hpad * nf)
        g = peer * rpd + inner
        for n, (y0, ny) in enumerate(cuts):
            g = jnp.where(piece == n, g + y0, g)
        cell = jnp.where(g < band, fy_ref[0] + g, fy_ref[1] + g - band)
        cosine, sine = turn(2 * (sv_ref[f] + b) * cell, mod)
        wide = jnp.concatenate([cosine, sine], axis=1) * F32(scale)
        hi, lo = split(wide)
        e_ref[pl.ds(first, block), pl.ds(0, 2 * depth)] = hi
        e_ref[pl.ds(first, block), pl.ds(2 * depth, 2 * depth)] = lo
        e_ref[pl.ds(first, block), pl.ds(4 * depth, 2 * depth)] = hi
        return carry

    zcopies = [[] for _ in cuts]
    for n in range(len(cuts)):
        for copy in sends[n]:
            copy.wait()
        transform(n)
    lax.fori_loop(0, SG // block, v_step, 0)

    flip = lax.broadcasted_iota(I32, (HALF, HALF), 0) + lax.broadcasted_iota(I32, (HALF, HALF), 1)
    flip = jnp.where(flip == HALF - 1, F32(1.0), F32(0.0)).astype(BF16)
    gcopies = []
    for n, (y0, ny) in enumerate(cuts):
        acc = part[n, 0]
        for d, copy in zcopies[n]:
            copy.wait()
            acc = acc + zrecv[n, d]
        pieces = []
        for m in range(2):
            hi, lo = split(acc[:, m * SG + HALF:(m + 1) * SG])
            pieces += [mm(hi, flip) + mm(lo, flip), acc[:, m * SG:m * SG + HALF]]
        total = jnp.concatenate(pieces, axis=1)
        options = [total[s * ny:(s + 1) * ny] for s in range(COLS_DEV)]
        group = []
        for d in range(1, nf):
            peer = partner(f, nf, d)
            chosen = options[0]
            for s in range(1, COLS_DEV):
                chosen = jnp.where(sc_ref[peer] == s, options[s], chosen)
            gsend[n, d, pl.ds(0, ny), :] = chosen
            copy = pltpu.make_async_remote_copy(
                src_ref=gsend.at[n, d], dst_ref=gat.at[n, f],
                send_sem=s_g.at[n, d], recv_sem=r_g.at[n, d],
                device_id=(peer, c), device_id_type=MESH,
            )
            copy.start()
            gcopies.append(copy)
        chosen = options[0]
        for s in range(1, COLS_DEV):
            chosen = jnp.where(sc_ref[f] == s, options[s], chosen)
        gat[n, f, pl.ds(0, ny), :] = chosen
    for copy in gcopies:
        copy.wait()
    for n, (y0, ny) in enumerate(cuts):
        for j in range(nf):
            h_ref[pl.ds((n * nf + j) * hpad, ny), :] = gat[n, j, pl.ds(0, ny), :]


def v_kernel(h_ref, e_ref, out_ref, rhs):
    @pl.when(pl.program_id(0) == 0)
    def _():
        k = h_ref.shape[0]
        hi, lo = split(h_ref[...])
        for n, h in enumerate((hi, hi, lo)):
            rhs[pl.ds(2 * n * k, k), :] = h
            rhs[pl.ds((2 * n + 1) * k, k), pl.ds(0, SG)] = h[:, SG:]
            rhs[pl.ds((2 * n + 1) * k, k), pl.ds(SG, SG)] = -h[:, :SG]

    out_ref[...] = mm(e_ref[...], rhs[...])


def per_device(nf, nc, facets, facet_x, facet_y, col_u, slot_col, slot_v):
    width = facets.shape[-1]
    band = facets.shape[2]
    img = width * nc * nf
    rows = facets.shape[0] * band
    rpd = rows // nf
    ncol = COLS_DEV * nc
    cuts = ((0, rpd // 2), (rpd // 2, rpd - rpd // 2))
    most = rpd - rpd // 2
    hpad = 1 << (most - 1).bit_length()
    depth = len(cuts) * nf * hpad
    pieces = len(cuts)
    vm = pl.BlockSpec(memory_space=pltpu.VMEM)
    sm = pl.BlockSpec(memory_space=pltpu.SMEM)
    dma = pltpu.SemaphoreType.DMA
    h, e = pl.pallas_call(
        functools.partial(gather_kernel, nf, nc, img, band, cuts, hpad),
        out_shape=(
            jax.ShapeDtypeStruct((depth, 2 * SG), F32),
            jax.ShapeDtypeStruct((SG, 6 * depth), BF16),
        ),
        in_specs=[sm, sm, sm, sm, sm, pl.BlockSpec(memory_space=pltpu.HBM)],
        out_specs=(vm, vm),
        scratch_shapes=[
            pltpu.VMEM((rpd, 2, nf, width), F32),
            pltpu.VMEM((8, 128), I32),
            pltpu.VMEM((nf, 8, 128), I32),
            pltpu.VMEM((2, width, SG), BF16),
            pltpu.VMEM((2, ncol, width), F32),
            pltpu.VMEM((2, ncol, nf, SG), F32),
            pltpu.VMEM((2, 2 * COLS_DEV * most * nf, width), BF16),
            pltpu.VMEM((pieces, nc, COLS_DEV * most, 2 * SG), F32),
            pltpu.VMEM((pieces, nc, COLS_DEV * most, 2 * SG), F32),
            pltpu.VMEM((pieces, nf, most, 2 * SG), F32),
            pltpu.VMEM((pieces, nf, most, 2 * SG), F32),
            dma((pieces, nf)), dma((pieces, nf)), dma((nf,)), dma((nf,)),
            dma((pieces, nc)), dma((pieces, nc)), dma((pieces, nf)), dma((pieces, nf)),
            dma((pieces + 1,)),
        ],
        compiler_params=pltpu.CompilerParams(
            collective_id=0, has_side_effects=True, vmem_limit_bytes=24 << 20
        ),
        name="gather_columns",
    )(facet_x, facet_y, col_u, slot_col[0], slot_v[0], facets.reshape(rows, 2, width))
    tile = 128
    out = pl.pallas_call(
        v_kernel,
        grid=(SG // tile,),
        out_shape=jax.ShapeDtypeStruct((SG, 2 * SG), F32),
        in_specs=[
            pl.BlockSpec((depth, 2 * SG), lambda i: (0, 0)),
            pl.BlockSpec((tile, 6 * depth), lambda i: (i, 0)),
        ],
        out_specs=pl.BlockSpec((tile, 2 * SG), lambda i: (i, 0)),
        scratch_shapes=[pltpu.VMEM((6 * depth, 2 * SG), BF16)],
        compiler_params=pltpu.CompilerParams(vmem_limit_bytes=24 << 20),
        name="v_transform",
    )(h, e)
    return out[None, None]


def solution(mesh):
    placed = (
        P(None, "facet", None, None, "col"),
        P("facet"),
        P(),
        P(),
        P("col", None),
        P("col", None),
    )
    return jax.shard_map(
        functools.partial(per_device, mesh.shape["facet"], mesh.shape["col"]),
        mesh=mesh,
        in_specs=placed,
        out_specs=P("col", "facet", None, None),
        check_vma=False,
    )
```

time: 36 us -> 31.4 us (0.87)
  Pallas kernels: 33.7 us -> 26.9 us
  local copies, waits for them, and re-layouts: 1.32 us -> 3.61 us
    pallas_call x1, Pallas kernels: 29.2 us -> 24.3 us  [per_device(): pl.pallas_call(functools.partial(gather_kernel, nf, nc, img, band, cuts,...]
    unnamed x0 -> x10, local copies, waits for them, and re-layouts: none -> 3.61 us
    pallas_call x1, Pallas kernels: 4.52 us -> 2.65 us  [per_device(): pl.pallas_call(v_kernel, grid=(SG // tile,), out_shape=jax.ShapeDtypeStru...]
    broadcast_in_dim x1 -> x0, local copies, waits for them, and re-layouts: 1.32 us -> none  [per_device(): col_u[:, None]]
where the time goes in v2:
time: 31.4 us; the launch traced here: 31.2 us
  Pallas kernels  26.9 us (86%)
  local copies, waits for them, and re-layouts  3.61 us (11%)
  between operations  0.67 us (2%)
    pallas_call x1, Pallas kernels, per_device(): pl.pallas_call(functools.partial(gather_kernel, nf, nc, img, band, cuts,...  24.3 us
    unnamed x10, local copies, waits for them, and re-layouts  3.61 us
    pallas_call x1, Pallas kernels, per_device(): pl.pallas_call(v_kernel, grid=(SG // tile,), out_shape=jax.ShapeDtypeStru...  2.65 us

profile of v2, /device:TPU:0, one launch (start us, length us, event | category | flops | bytes accessed | tf_op | source)
XLA Modules:
  0.0 31.2 jit_solution(11381468171129410268)
XLA Ops:
  0.7 0.0 copy-start
  0.7 1.0 %copy-done = f32[2,1,24,2,1024]{4,3,2,1,0:T(2,128)S(1)} copy-done((f32[2,1,24,2,1024]{4,3,2,1,0:T(2,128)S(1)}, f32[2,1,24,2,1024]{4,3,2,1,0:T(2,128)}, u32[]{:S(2)}) %copy-start) | copy-done | bytes 393240
  1.6 0.0 copy-start.1
  1.7 0.7 %copy-done.1 = s32[2]{0:T(128)S(1)} copy-done((s32[2]{0:T(128)S(1)}, s32[2]{0:T(128)}, u32[]{:S(2)}) %copy-start.1) | copy-done | bytes 32
  2.3 0.0 copy-start.2
  2.3 0.7 %copy-done.2 = s32[8]{0:T(128)S(1)} copy-done((s32[8]{0:T(128)S(1)}, s32[8]{0:T(128)}, u32[]{:S(2)}) %copy-start.2) | copy-done | bytes 56
  3.0 0.0 copy-start.3
  3.0 0.7 %copy-done.3 = s32[1,8]{1,0:T(1,128)S(1)} copy-done((s32[1,8]{1,0:T(1,128)S(1)}, s32[1,8]{1,0:T(1,128)}, u32[]{:S(2)}) %copy-start.3) | copy-done | bytes 56
  3.6 0.0 copy-start.4
  3.6 0.7 %copy-done.4 = s32[1,8]{1,0:T(1,128)S(1)} copy-done((s32[1,8]{1,0:T(1,128)S(1)}, s32[1,8]{1,0:T(1,128)}, u32[]{:S(2)}) %copy-start.4) | copy-done | bytes 56
  4.3 24.3 %gather_columns.1 = (f32[64,1024]{1,0:T(8,128)S(1)}, bf16[512,384]{1,0:T(8,128)(2,1)S(1)}) custom-call(s32[1]{0:T(128)S(6)} %copy.7.fx_ref, s32[2]{0:T(128)S(1)} %copy-done.1, s32[8]{0:T(128)S(1)} %copy-done.2, s32[8]{0:T(128)S(1)} %bitcast.5, s32[8]{0:T(128)S(1)} %bitcast.6, f32[48,2,1024]{2,1,0:T(2,128)S(1)} %bitcast.4), custom_call_target="tpu_custom_call" | custom-call | tf_op jit(solution)/shard_map/gather_columns/pallas_call | solution.py:296
  28.6 2.7 %v_transform.1 = f32[512,1024]{1,0:T(8,128)} custom-call(f32[64,1024]{1,0:T(8,128)S(1)} %get-tuple-element.7.h_ref, bf16[512,384]{1,0:T(8,128)(2,1)S(1)} %get-tuple-element.8.e_ref), custom_call_target="tpu_custom_call" | custom-call | tf_op jit(solution)/shard_map/v_transform/pallas_call | solution.py:326
Async XLA Ops:
  0.7 1.0 %copy-start = (f32[2,1,24,2,1024]{4,3,2,1,0:T(2,128)S(1)}, f32[2,1,24,2,1024]{4,3,2,1,0:T(2,128)}, u32[]{:S(2)}) copy-start(f32[2,1,24,2,1024]{4,3,2,1,0:T(2,128)} %param.6) | copy-start | bytes 1179652
  1.6 0.7 %copy-start.1 = (s32[2]{0:T(128)S(1)}, s32[2]{0:T(128)}, u32[]{:S(2)}) copy-start(s32[2]{0:T(128)} %fy_ref.1) | copy-start | bytes 28
  2.3 0.7 %copy-start.2 = (s32[8]{0:T(128)S(1)}, s32[8]{0:T(128)}, u32[]{:S(2)}) copy-start(s32[8]{0:T(128)} %u_ref.1) | copy-start | bytes 100
  3.0 0.7 %copy-start.3 = (s32[1,8]{1,0:T(1,128)S(1)}, s32[1,8]{1,0:T(1,128)}, u32[]{:S(2)}) copy-start(s32[1,8]{1,0:T(1,128)} %param.10) | copy-start | bytes 100
  3.6 0.7 %copy-start.4 = (s32[1,8]{1,0:T(1,128)S(1)}, s32[1,8]{1,0:T(1,128)}, u32[]{:S(2)}) copy-start(s32[1,8]{1,0:T(1,128)} %param.11) | copy-start | bytes 100

commit v3 on v2

--- a/solution.py
+++ b/solution.py
@@ -58,10 +58,11 @@
 
 def gather_kernel(
     nf, nc, img, band, cuts, hpad,
-    fx_ref, fy_ref, u_ref, sc_ref, sv_ref, facets_ref,
+    fx_ref, fy_hbm, u_hbm, sc_hbm, sv_hbm, facets_ref,
     h_ref, e_ref,
     cells, fxs, fxall, table, premod, phase, zbuf, part, zrecv, gsend, gat,
-    s_a2a, r_a2a, s_fx, r_fx, s_z, r_z, s_g, r_g, l_sem,
+    fy_ref, u_ref, sc_ref, sv_ref,
+    s_a2a, r_a2a, s_fx, r_fx, s_z, r_z, s_g, r_g, l_sem, i_sem,
 ):
     f = lax.axis_index("facet")
     c = lax.axis_index("col")
@@ -72,13 +73,22 @@
     ncol = COLS_DEV * nc
     depth = len(cuts) * nf * hpad
 
-    fxs[...] = jnp.full(fxs.shape, fx_ref[0], I32)
+    numbers = []
+    for i, (src, dst) in enumerate((
+        (fy_hbm, fy_ref), (u_hbm, u_ref), (sc_hbm, sc_ref), (sv_hbm, sv_ref)
+    )):
+        copy = pltpu.make_async_copy(src, dst, i_sem.at[i])
+        copy.start()
+        numbers.append(copy)
     barrier = pltpu.get_barrier_semaphore()
     for d in range(1, nf):
         pl.semaphore_signal(barrier, inc=1, device_id=(partner(f, nf, d), c), device_id_type=MESH)
     for d in range(1, nc):
         pl.semaphore_signal(barrier, inc=1, device_id=(f, partner(c, nc, d)), device_id_type=MESH)
 
+    for copy in numbers:
+        copy.wait()
+    fxs[...] = jnp.full(fxs.shape, fx_ref[0], I32)
     start = c * width
     xs = lax.broadcasted_iota(I32, (ncol, width), 1) + start
     row = lax.broadcasted_iota(I32, (ncol, width), 0)
@@ -291,7 +301,6 @@
     depth = len(cuts) * nf * hpad
     pieces = len(cuts)
     vm = pl.BlockSpec(memory_space=pltpu.VMEM)
-    sm = pl.BlockSpec(memory_space=pltpu.SMEM)
     dma = pltpu.SemaphoreType.DMA
     h, e = pl.pallas_call(
         functools.partial(gather_kernel, nf, nc, img, band, cuts, hpad),
@@ -299,7 +308,7 @@
             jax.ShapeDtypeStruct((depth, 2 * SG), F32),
             jax.ShapeDtypeStruct((SG, 6 * depth), BF16),
         ),
-        in_specs=[sm, sm, sm, sm, sm, pl.BlockSpec(memory_space=pltpu.HBM)],
+        in_specs=[pl.BlockSpec(memory_space=pltpu.SMEM)] + [pl.BlockSpec(memory_space=pltpu.HBM)] * 5,
         out_specs=(vm, vm),
         scratch_shapes=[
             pltpu.VMEM((rpd, 2, nf, width), F32),
@@ -313,15 +322,20 @@
             pltpu.VMEM((pieces, nc, COLS_DEV * most, 2 * SG), F32),
             pltpu.VMEM((pieces, nf, most, 2 * SG), F32),
             pltpu.VMEM((pieces, nf, most, 2 * SG), F32),
+            pltpu.SMEM((2,), I32), pltpu.SMEM((ncol,), I32),
+            pltpu.SMEM((nf,), I32), pltpu.SMEM((nf,), I32),
             dma((pieces, nf)), dma((pieces, nf)), dma((nf,)), dma((nf,)),
             dma((pieces, nc)), dma((pieces, nc)), dma((pieces, nf)), dma((pieces, nf)),
-            dma((pieces + 1,)),
+            dma((pieces + 1,)), dma((4,)),
         ],
         compiler_params=pltpu.CompilerParams(
             collective_id=0, has_side_effects=True, vmem_limit_bytes=24 << 20
         ),
         name="gather_columns",
-    )(facet_x, facet_y, col_u, slot_col[0], slot_v[0], facets.reshape(rows, 2, width))
+    )(facet_x, *(
+        pltpu.with_memory_space_constraint(z, pltpu.HBM)
+        for z in (facet_y, col_u, slot_col[0], slot_v[0], facets.reshape(rows, 2, width))
+    ))
     tile = 128
     out = pl.pallas_call(
         v_kernel,

time: 31.4 us -> 27.2 us (0.87)
  local copies, waits for them, and re-layouts: 3.61 us -> 0 us
  Pallas kernels: 26.9 us -> 26.4 us
    unnamed x10 -> x0, local copies, waits for them, and re-layouts: 3.61 us -> none
    pallas_call x1, Pallas kernels: 24.3 us -> 23.8 us  [per_device(): pl.pallas_call(functools.partial(gather_kernel, nf, nc, img, band, cuts,...]
where the time goes in v3:
time: 27.2 us; the launch traced here: 27.1 us
  Pallas kernels  26.4 us (97%)
  between operations  0.66 us (2%)
    pallas_call x1, Pallas kernels, per_device(): pl.pallas_call(functools.partial(gather_kernel, nf, nc, img, band, cuts,...  23.8 us
    pallas_call x1, Pallas kernels, per_device(): pl.pallas_call(v_kernel, grid=(SG // tile,), out_shape=jax.ShapeDtypeStru...  2.64 us

profile of v3, /device:TPU:0, one launch (start us, length us, event | category | flops | bytes accessed | tf_op | source)
XLA Modules:
  0.0 27.1 jit_solution(7627703908486035258)
XLA Ops:
  0.7 23.8 %gather_columns.1 = (f32[64,1024]{1,0:T(8,128)S(1)}, bf16[512,384]{1,0:T(8,128)(2,1)S(1)}) custom-call(s32[1]{0:T(128)S(6)} %copy.7.fx_ref, s32[2]{0:T(128)} %fy_hbm.1, s32[8]{0:T(128)} %u_hbm.1, s32[8]{0:T(128)} %bitcast.5, s32[8]{0:T(128)} %bitcast.6, f32[48,2,1024]{2,1,0:T(2,128)} %bitcast.4), custom_call_target="tpu_custom_call" | custom-call | tf_op jit(solution)/shard_map/gather_columns/pallas_call | solution.py:305
  24.4 2.6 %v_transform.1 = f32[512,1024]{1,0:T(8,128)} custom-call(f32[64,1024]{1,0:T(8,128)S(1)} %get-tuple-element.7.h_ref, bf16[512,384]{1,0:T(8,128)(2,1)S(1)} %get-tuple-element.8.e_ref), custom_call_target="tpu_custom_call" | custom-call | tf_op jit(solution)/shard_map/v_transform/pallas_call | solution.py:340

commit v4 on v3

--- a/solution.py
+++ b/solution.py
@@ -73,6 +73,7 @@
     ncol = COLS_DEV * nc
     depth = len(cuts) * nf * hpad
 
+    fxs[...] = jnp.full(fxs.shape, fx_ref[0], I32)
     numbers = []
     for i, (src, dst) in enumerate((
         (fy_hbm, fy_ref), (u_hbm, u_ref), (sc_hbm, sc_ref), (sv_hbm, sv_ref)
@@ -86,19 +87,6 @@
     for d in range(1, nc):
         pl.semaphore_signal(barrier, inc=1, device_id=(f, partner(c, nc, d)), device_id_type=MESH)
 
-    for copy in numbers:
-        copy.wait()
-    fxs[...] = jnp.full(fxs.shape, fx_ref[0], I32)
-    start = c * width
-    xs = lax.broadcasted_iota(I32, (ncol, width), 1) + start
-    row = lax.broadcasted_iota(I32, (ncol, width), 0)
-    uv = jnp.zeros((ncol, width), I32)
-    for i in range(ncol):
-        uv = jnp.where(row == i, u_ref[i], uv)
-    pc, ps = turn((2 * uv + (SG - 1)) * xs, mod)
-    premod[0] = pc
-    premod[1] = ps
-    h_ref[...] = jnp.zeros_like(h_ref)
     pl.semaphore_wait(barrier, nf + nc - 2)
 
     small = []
@@ -133,6 +121,18 @@
         group.append(copy)
         sends.append(group)
 
+    for copy in numbers:
+        copy.wait()
+    start = c * width
+    xs = lax.broadcasted_iota(I32, (ncol, width), 1) + start
+    row = lax.broadcasted_iota(I32, (ncol, width), 0)
+    uv = jnp.zeros((ncol, width), I32)
+    for i in range(ncol):
+        uv = jnp.where(row == i, u_ref[i], uv)
+    pc, ps = turn((2 * uv + (SG - 1)) * xs, mod)
+    premod[0] = pc
+    premod[1] = ps
+    h_ref[...] = jnp.zeros_like(h_ref)
     block = 64
 
     def table_step(i, carry):

time: 27.2 us -> 27.2 us (level)
  no operation moved by 1% of the time
where the time goes in v4:
time: 27.2 us; the launch traced here: 27.1 us
  Pallas kernels  26.4 us (97%)
  between operations  0.66 us (2%)
    pallas_call x1, Pallas kernels, per_device(): pl.pallas_call(functools.partial(gather_kernel, nf, nc, img, band, cuts,...  23.8 us
    pallas_call x1, Pallas kernels, per_device(): pl.pallas_call(v_kernel, grid=(SG // tile,), out_shape=jax.ShapeDtypeStru...  2.64 us

profile of v4, /device:TPU:0, one launch (start us, length us, event | category | flops | bytes accessed | tf_op | source)
XLA Modules:
  0.0 27.1 jit_solution(10872432005364684699)
XLA Ops:
  0.7 23.8 %gather_columns.1 = (f32[64,1024]{1,0:T(8,128)S(1)}, bf16[512,384]{1,0:T(8,128)(2,1)S(1)}) custom-call(s32[1]{0:T(128)S(6)} %copy.7.fx_ref, s32[2]{0:T(128)} %fy_hbm.1, s32[8]{0:T(128)} %u_hbm.1, s32[8]{0:T(128)} %bitcast.5, s32[8]{0:T(128)} %bitcast.6, f32[48,2,1024]{2,1,0:T(2,128)} %bitcast.4), custom_call_target="tpu_custom_call" | custom-call | tf_op jit(solution)/shard_map/gather_columns/pallas_call | solution.py:305
  24.4 2.6 %v_transform.1 = f32[512,1024]{1,0:T(8,128)} custom-call(f32[64,1024]{1,0:T(8,128)S(1)} %get-tuple-element.7.h_ref, bf16[512,384]{1,0:T(8,128)(2,1)S(1)} %get-tuple-element.8.e_ref), custom_call_target="tpu_custom_call" | custom-call | tf_op jit(solution)/shard_map/v_transform/pallas_call | solution.py:340
